TPU v7x, 32 devices: a whole 2x2x4 slice. The times are simulated.
32 devices in a mesh: dp: 2 (over y), tensor: 8 (over z, core), fisher: 2 (over x).
Axes of the slice: x: 2, y: 2, z: 4, core: 2. Of those that a mesh axis runs over, the one named last changes fastest.
Arguments:
- train_inputs: bfloat16 [44, 257, 1280], P('dp', None, 'fisher'), may hold values from -6 to 6
- train_cotangents: bfloat16 [44, 257, 3840], P('dp', None, 'tensor'), may hold values from -6 to 6
- train_ids: int32 [44], P('dp'), may hold values from 0 to 15
- query_projection_inputs: bfloat16 [8, 257, 1280], P('tensor', None, 'fisher'), may hold values from -6 to 6
- query_output_cotangents: bfloat16 [8, 257, 3840], P('tensor'), may hold values from -6 to 6
- query_ids: int32 [8], replicated, may hold values from 0 to 15
- fisher_diagonal_weight: bfloat16 [2, 3840, 1280], P(None, 'tensor', 'fisher'), may hold values from 0.049804688 to 2
- layer_index: int32 [16], replicated, may hold values from 0 to 1
Outputs:
- influence: float32 [16, 16, 16], P(('dp', 'fisher'), None, 'tensor')
All inputs are finite; a program needn't handle non-finite values.
Results may differ from a plain program's by a relative error of at most 0.004.
Values may be sent and summed in bfloat16 or wider, within the bound.
A program may use at most 128 MiB of HBM per device.

v0:
```python
import math

import jax
import jax.numpy as jnp
from jax import lax
from jax.sharding import PartitionSpec as P

D = 1280
HEAD_DIM = 80
SEQ = 257
TID_DEV = 4
QIDS = 16


def local(
    train_inputs,
    train_cotangents,
    train_ids,
    query_projection_inputs,
    query_output_cotangents,
    query_ids,
    fisher_diagonal_weight,
    layer_index,
):
    head_width = 3 * HEAD_DIM
    scale_factor = 1.0 / (SEQ * math.sqrt(3 * HEAD_DIM * D))
    local_heads = train_cotangents.shape[2] // head_width
    count_train = train_inputs.shape[0]
    half_width = train_inputs.shape[2]
    stored_count = fisher_diagonal_weight.shape[0]
    head_first = lax.axis_index("tensor") * local_heads
    own_layers = lax.dynamic_slice_in_dim(layer_index, head_first, local_heads, 0)
    picked = own_layers[None, :] == jnp.arange(stored_count, dtype=jnp.int32)[:, None]
    stacked = fisher_diagonal_weight.reshape(stored_count, local_heads, head_width, half_width)
    chosen = jnp.sum(jnp.where(picked[:, :, None, None], stacked.astype(jnp.float32), 0.0), axis=0)
    fisher_layer = chosen.reshape(local_heads * head_width, half_width).astype(jnp.bfloat16)
    train_grad = jnp.einsum(
        "nsr,nsd->nrd", train_cotangents, train_inputs, preferred_element_type=jnp.float32
    ).astype(jnp.bfloat16)
    fisher_local = fisher_layer.astype(jnp.float32)
    received = lax.all_to_all(
        query_output_cotangents, "tensor", split_axis=2, concat_axis=0, tiled=True
    )
    block_grad = jnp.einsum(
        "kzo,kzj->koj",
        received,
        lax.all_gather(query_projection_inputs, "tensor", axis=0, tiled=True),
        preferred_element_type=jnp.float32,
    )
    weighted = (fisher_local[None] * block_grad).astype(jnp.bfloat16)
    count_query = weighted.shape[0]
    train_flat = train_grad.reshape(count_train, local_heads, head_width * half_width)
    query_flat = weighted.reshape(count_query, local_heads, head_width * half_width)
    scores = (
        lax.dot_general(
            train_flat, query_flat, (((2,), (2,)), ((1,), (1,))), preferred_element_type=jnp.float32
        )
        * scale_factor
    )
    total_ids = TID_DEV * lax.axis_size("dp") * lax.axis_size("fisher")
    train_hot = (train_ids[:, None] == jnp.arange(total_ids, dtype=jnp.int32)[None, :]).astype(
        jnp.float32
    )
    query_hot = (query_ids[:, None] == jnp.arange(QIDS, dtype=jnp.int32)[None, :]).astype(
        jnp.float32
    )
    buckets = jnp.einsum(
        "hnm,na,mb->hab", scores, train_hot, query_hot, precision=lax.Precision.HIGHEST
    )
    shares = lax.psum_scatter(buckets, ("dp", "fisher"), scatter_dimension=1, tiled=True)
    return jnp.transpose(shares, (1, 2, 0))


def solution(mesh):
    in_specs = (
        P("dp", None, "fisher"),
        P("dp", None, "tensor"),
        P("dp"),
        P("tensor", None, "fisher"),
        P("tensor", None, None),
        P(),
        P(None, "tensor", "fisher"),
        P(),
    )
    out_specs = P(("dp", "fisher"), None, "tensor")
    return jax.shard_map(local, mesh=mesh, in_specs=in_specs, out_specs=out_specs, check_vma=False)
```

profile of v0, /device:TPU:0, one launch (start us, length us, event | category | flops | bytes accessed | tf_op | source)
XLA Modules:
  0.0 169.4 jit_solution(9806941971329295735)
XLA Ops:
  6.5 0.0 all-gather.2.cloned.1.call-start
  6.5 0.7 all-gather.2.cloned.1.call-update
  7.3 12.2 %copy.12 = bf16[1,257,3840]{1,0,2:T(2,128)(2,1)} copy(bf16[1,257,3840]{2,1,0:T(8,128)(2,1)} %param.12) | data formatting | bytes 3947520 | tf_op args[4]
  19.5 0.5 broadcast.15
  20.0 24.6 %reduce.1 = bf16[3840,257]{1,0:T(8,128)(2,1)S(1)} reduce(bf16[3840,1,257]{2,1,0:T(2,128)(2,1)} %bitcast.29, bf16[]{:T(256)} %broadcast.15), dimensions={1}, to_apply=%bitcast.22.reduce_sub_computation | reduce | bytes 3947522
  44.6 0.0 copy-start.1
  44.6 7.1 %reshape.44 = bf16[8,2,61680]{2,1,0:T(2,128)(2,1)} reshape(bf16[3840,257]{1,0:T(8,128)(2,1)S(1)} %reduce.1) | data formatting | bytes 3947520
  51.7 6.4 %all-to-all-start = ((bf16[8,2,61680]{2,1,0:T(2,128)(2,1)}), bf16[8,2,61680]{2,1,0:T(2,128)(2,1)S(1)}, u32[]{:S(2)}, u32[]{:S(2)}) async-start(bf16[8,2,61680]{2,1,0:T(2,128)(2,1)} %reshape.44), calls=%async_computation | async-start | bytes 3948544 | tf_op jit(solution)/shard_map/all_to_all | solution.py:41
  58.1 0.0 copy-done.1
  58.1 0.1 dynamic_slice.3
  58.2 0.1 broadcast_in_dim.24
  58.3 0.1 broadcast_in_dim.25
  58.4 1.6 select_reduce_fusion
  60.0 1.2 convert_element_type.36
  61.2 15.5 %convolution_convert_fusion = bf16[22,480,640]{2,1,0:T(8,128)(2,1)} fusion(bf16[22,257,480]{2,1,0:T(8,128)(2,1)} %param.9, bf16[22,257,640]{2,1,0:T(8,128)(2,1)} %param.8), kind=kOutput, calls=%fused_computation.2 | convolution fusion | flops 3480576000 | bytes 26181760 | tf_op jit(solution)/shard_map/nsr,nsd->nrd/dot_general | solution.py:37
  76.7 0.0 copy-start.3
  76.7 18.1 %reshape.35 = bf16[22,2,153600]{2,1,0:T(2,128)(2,1)} reshape(bf16[22,480,640]{2,1,0:T(8,128)(2,1)} %convolution_convert_fusion) | data formatting | bytes 27033600 | tf_op jit(solution)/shard_map/reshape | solution.py:52
  94.7 0.0 copy-done.3
  94.7 0.6 dynamic-slice
  96.0 8.5 %all-to-all-done = bf16[8,2,61680]{2,1,0:T(2,128)(2,1)S(1)} async-done(((bf16[8,2,61680]{2,1,0:T(2,128)(2,1)}), bf16[8,2,61680]{2,1,0:T(2,128)(2,1)S(1)}, u32[]{:S(2)}, u32[]{:S(2)}) %all-to-all-start) | async-done | bytes 1973792 | tf_op jit(solution)/shard_map/all_to_all | solution.py:41
  104.5 8.2 %reshape.45 = bf16[3840,1,257]{2,1,0:T(2,128)(2,1)} reshape(bf16[8,2,61680]{2,1,0:T(2,128)(2,1)S(1)} %all-to-all-done) | data formatting | bytes 3947520
  112.7 3.2 %copy.22 = bf16[1,257,3840]{1,2,0:T(8,128)(2,1)S(1)} copy(bf16[1,257,3840]{1,0,2:T(2,128)(2,1)} %bitcast.30) | data formatting | bytes 3947520
  115.9 2.6 %copy.14 = bf16[1,257,8,480]{3,1,2,0:T(8,128)(2,1)} copy(bf16[1,257,8,480]{1,3,2,0:T(8,128)(2,1)S(1)} %bitcast.31) | data formatting | bytes 3947520 | tf_op jit(solution)/shard_map/all_to_all | solution.py:41
  118.5 0.0 all-gather.2.cloned.1.call-done
  118.5 8.0 %multiply_convert_fusion = bf16[8,480,640]{2,1,0:T(8,128)(2,1)} fusion(f32[480,640]{1,0:T(8,128)} %convert_element_type.36, bf16[8,257,640]{2,1,0:T(8,128)(2,1)} %all-gather.2.cloned.1.call-done, bf16[1,257,8,480]{3,1,2,0:T(8,128)(2,1)} %copy.14), kind=kOutput, calls=%fused_computation.3 | convolution fusion | flops 1268121600 | bytes 10749440 | tf_op jit(solution)/shard_map/kzo,kzj->koj/dot_general | solution.py:44
  126.5 7.4 %reshape.36 = bf16[8,2,153600]{2,1,0:T(2,128)(2,1)} reshape(bf16[8,480,640]{2,1,0:T(8,128)(2,1)} %multiply_convert_fusion) | data formatting | bytes 9830400 | tf_op jit(solution)/shard_map/reshape | solution.py:53
  133.8 0.0 copy-start
  133.8 0.0 copy-start.2
  133.8 11.7 %fusion.9 = f32[22,16]{0,1:T(8,128)S(1)} fusion(bf16[8,2,153600]{2,1,0:T(2,128)(2,1)} %reshape.36, bf16[22,2,153600]{2,1,0:T(2,128)(2,1)} %reshape.35), kind=kOutput, calls=%fused_computation.10 | convolution fusion | flops 108134752 | bytes 18433408 | tf_op jit(solution)/shard_map/dot_general | solution.py:55
  145.6 0.0 copy-done
  145.6 0.1 convolution_bitcast_fusion.1
  145.7 0.0 copy-done.2
  145.7 0.2 convolution_bitcast_fusion
  145.9 16.0 %all-reduce = f32[2,16,16]{2,1,0:T(8,128)S(1)} all-reduce(f32[2,16,16]{2,1,0:T(8,128)S(1)} %convolution_bitcast_fusion), channel_id=2, replica_groups=mesh['dp'=2,'tensor'=8,'fisher'=2] {'dp','fisher'}, use_global_device_ids=true, to_apply=%region_1.2.clone | all-reduce | flops 512 | bytes 4096
  162.0 0.6 copy.17
  (2 shorter events, 0.0 us)
Async XLA Ops:
  6.5 111.9 %all-gather.2.cloned.1.call-start = ((), (), s32[]{:S(2)}) async-start(), calls=%async_computation.1 | async-start | bytes 3041280 | tf_op jit(solution)/shard_map/all_gather | solution.py:47
  44.6 13.5 %copy-start.1 = (s32[16]{0:T(128)S(1)}, s32[16]{0:T(128)}, u32[]{:S(2)}) copy-start(s32[16]{0:T(128)} %param.15) | copy-start | bytes 196
  51.7 52.8 %all-to-all-start = ((bf16[8,2,61680]{2,1,0:T(2,128)(2,1)}), bf16[8,2,61680]{2,1,0:T(2,128)(2,1)S(1)}, u32[]{:S(2)}, u32[]{:S(2)}) async-start(bf16[8,2,61680]{2,1,0:T(2,128)(2,1)} %reshape.44), calls=%async_computation | async-start | bytes 3948544 | tf_op jit(solution)/shard_map/all_to_all | solution.py:41
  76.7 18.1 %copy-start.3 = (u32[32]{0:T(128)S(1)}, u32[32]{0:T(128)}, u32[]{:S(2)}) copy-start(u32[32]{0:T(128)} %constant.20) | copy-start | bytes 388
  133.8 11.7 %copy-start = (s32[22]{0:T(128)S(1)}, s32[22]{0:T(128)}, u32[]{:S(2)}) copy-start(s32[22]{0:T(128)} %param.10) | copy-start | bytes 268
  133.8 11.9 %copy-start.2 = (s32[8]{0:T(128)S(1)}, s32[8]{0:T(128)}, u32[]{:S(2)}) copy-start(s32[8]{0:T(128)} %param.13) | copy-start | bytes 100
Sparse Core Ops, SparseCore 0:
  9.0 37.1 all-gather.1
where the time goes:
time: 171 us; the launch traced here: 169 us
  local copies, waits for them, and re-layouts  60.8 us (36%)
  matrix products  35.6 us (21%)
  other arithmetic  27.4 us (16%)
  blocking collectives  16 us (9%)
  between operations  14.1 us (8%)
  waiting for transfers between devices  9.24 us (5%)
  starting transfers between devices  6.37 us (4%)
    unnamed x14, local copies, waits for them, and re-layouts  31.9 us
    unnamed x1, other arithmetic  24.6 us
    reshape x1, local copies, waits for them, and re-layouts, local(): train_grad.reshape(count_train, local_heads, head_width * half_width)  18.1 us
    unnamed x1, blocking collectives  16 us
    dot_general x1, matrix products, local(): jnp.einsum('nsr,nsd->nrd', train_cotangents, train_inputs, preferred_elem...  15.5 us
    dot_general x1, matrix products, local(): lax.dot_general(train_flat, query_flat, (((2,), (2,)), ((1,), (1,))), pre...  11.7 us
    all_to_all x1, waiting for transfers between devices, local(): lax.all_to_all(query_output_cotangents, 'tensor', split_axis=2, concat_ax...  8.53 us
    dot_general x1, matrix products, local(): jnp.einsum('kzo,kzj->koj', received, lax.all_gather(query_projection_inpu...  7.99 us
  transfers between devices with their start and end apart: 2, of which 1 were waited for; matrix products, arithmetic and copies ran while one was open for 56% of the time, Pallas kernels for 0%

commit v1 on v0

v1 whole, which is shorter than its diff:
```python
import functools
import math

import jax
import jax.numpy as jnp
from jax import lax
from jax.experimental import pallas as pl
from jax.experimental.pallas import tpu as pltpu
from jax.sharding import PartitionSpec as P

HEAD_DIM = 80
HEAD_WIDTH = 3 * HEAD_DIM
QIDS = 16
LANES = 128
RB = 16
MESH = pl.DeviceIdType.MESH
F32 = jnp.float32
BF16 = jnp.bfloat16
TN = (((0,), (0,)), ((), ()))
NT = (((1,), (1,)), ((), ()))


def kernel(
    sizes,
    layer_ref,
    tx_hbm,
    tc_hbm,
    qx_hbm,
    qc_hbm,
    fw_hbm,
    tid_ref,
    qid_ref,
    out_ref,
    tx,
    tc,
    grad,
    qc,
    qx,
    weighted,
    fw,
    block,
    acc,
    part,
    got,
    tx_sem,
    tc_sem,
    fw_sem,
    own_sem,
    qc_recv,
    qc_send,
    qx_recv,
    qx_send,
    part_send,
    part_recv,
):
    tensor_n, dp_n, fisher_n, win, ids_dev, scale = sizes
    count, seq, half = tx.shape
    width = tc.shape[2]
    heads = width // HEAD_WIDTH
    total_cols = qc_hbm.shape[2]
    stored = fw.shape[0]
    groups = dp_n * fisher_n
    chips = tensor_n // 2

    dp = lax.axis_index("dp")
    t = lax.axis_index("tensor")
    f = lax.axis_index("fisher")
    a = lax.rem(dp, 2)
    dp_other = dp + 1 - 2 * a
    f_other = 1 - f
    core = lax.rem(t, 2)
    t_other = t + 1 - 2 * core
    me = dp * fisher_n + f

    def start_of(dest):
        first = lax.min((dest * width) // LANES * LANES, total_cols - win)
        return pl.multiple_of(first, LANES)

    def window(dest):
        return qc_hbm.at[0, :, pl.ds(start_of(dest), win)]

    def remote(src, dst, send, recv, to):
        return pltpu.make_async_remote_copy(
            src_ref=src, dst_ref=dst, send_sem=send, recv_sem=recv, device_id=to, device_id_type=MESH
        )

    barrier = pltpu.get_barrier_semaphore()
    for k in range(1, tensor_n):
        pl.semaphore_signal(
            barrier, inc=1, device_id={"tensor": lax.rem(t + k, tensor_n)}, device_id_type=MESH
        )
    for d in range(1, groups):
        g = lax.rem(me + d, groups)
        pl.semaphore_signal(
            barrier,
            inc=1,
            device_id={"dp": g // fisher_n, "fisher": lax.rem(g, fisher_n)},
            device_id_type=MESH,
        )

    own_c = pltpu.make_async_copy(window(t), qc.at[t], own_sem.at[0])
    own_x = pltpu.make_async_copy(qx_hbm.at[0], qx.at[t], own_sem.at[1])
    load_f = pltpu.make_async_copy(fw_hbm, fw, fw_sem)

    def load_x(n):
        return pltpu.make_async_copy(tx_hbm.at[n], tx.at[n], tx_sem.at[n])

    def load_c(n):
        return pltpu.make_async_copy(tc_hbm.at[n], tc.at[n], tc_sem.at[n])

    own_c.start()
    own_x.start()

    @pl.loop(0, count)
    def _(n):
        load_x(n).start()
        load_c(n).start()

    load_f.start()
    pl.semaphore_wait(barrier, tensor_n - 1 + groups - 1)

    def on_line(k):
        return jnp.logical_and(a == k % 2, f == (k // 2) % 2)

    def qc_first(k):
        dest = lax.rem(t + tensor_n - k, tensor_n)
        return remote(window(dest), qc.at[t], qc_send.at[0, k], qc_recv.at[t], {"tensor": dest})

    def slot(k):
        return lax.rem(t + k, tensor_n)

    def qc_to_dp(k):
        m = slot(k)
        return remote(qc.at[m], qc.at[m], qc_send.at[1, k], qc_recv.at[m], {"dp": dp_other})

    def qc_to_fisher(k):
        m = slot(k)
        return remote(qc.at[m], qc.at[m], qc_send.at[2, k], qc_recv.at[m], {"fisher": f_other})

    def x_line(j, side):
        source_core = lax.rem(core + side, 2)
        return lax.rem(source_core + j, 2)

    def x_slot(j, side):
        return 2 * lax.rem(t // 2 + j, chips) + lax.rem(core + side, 2)

    def qx_first(j):
        dest = lax.rem(t + tensor_n - 2 * j, tensor_n)
        return remote(qx_hbm.at[0], qx.at[t], qx_send.at[0, j], qx_recv.at[t], {"tensor": dest})

    def qx_partner():
        return remote(qx_hbm.at[0], qx.at[t], qx_send.at[0, 0], qx_recv.at[t], {"tensor": t_other})

    def qx_to_partner(j):
        m = x_slot(j, 0)
        return remote(qx.at[m], qx.at[m], qx_send.at[1, j], qx_recv.at[m], {"tensor": t_other})

    def qx_to_dp(j):
        m = x_slot(j, 0)
        return remote(qx.at[m], qx.at[m], qx_send.at[2, j], qx_recv.at[m], {"dp": dp_other})

    x_order = list(range(1, chips))
    c_order = list(range(1, tensor_n))
    for i in range(max(len(x_order), len(c_order))):
        if i < len(c_order):
            k = c_order[i]

            @pl.when(on_line(k))
            def _(k=k):
                qc_first(k).start()

        if i < len(x_order):
            j = x_order[i]

            @pl.when(a == x_line(j, 0))
            def _(j=j):
                qx_first(j).start()

    qx_partner().start()

    def train(lo, hi):
        @pl.loop(lo, hi)
        def _(n):
            load_x(n).wait()
            load_c(n).wait()
            grad[n] = lax.dot_general(tc[n], tx[n], TN, preferred_element_type=F32).astype(BF16)

    def forward_c(k):
        @pl.when(on_line(k))
        def _():
            qc_to_dp(k).wait_recv()
            qc_to_dp(k).start()
            qc_to_fisher(k).start()

    def forward_x(j):
        @pl.when(a == x_line(j, 0))
        def _():
            qx_to_dp(j).wait_recv()
            qx_to_dp(j).start()
            qx_to_partner(j).start()

    half_c = (len(c_order) + 1) // 2
    cut = count // 3
    train(0, cut)
    for k in c_order[:half_c]:
        forward_c(k)
    for j in x_order[: (len(x_order) + 1) // 2]:
        forward_x(j)
    train(cut, 2 * cut)
    for k in c_order[half_c:]:
        forward_c(k)
    for j in x_order[(len(x_order) + 1) // 2 :]:
        forward_x(j)
    train(2 * cut, count)

    for k in c_order:

        @pl.when(jnp.logical_and(a != k % 2, f == (k // 2) % 2))
        def _(k=k):
            qc_to_fisher(k).wait_recv()
            qc_to_fisher(k).start()

    for j in x_order:

        @pl.when(a != x_line(j, 0))
        def _(j=j):
            qx_to_partner(j).wait_recv()
            qx_to_partner(j).start()

    for k in c_order:

        @pl.when(f != (k // 2) % 2)
        def _(k=k):
            qc_to_fisher(k).wait_recv()

    for j in range(chips):
        m = x_slot(j, 1)
        remote(qx.at[m], qx.at[m], qx_send.at[1, j], qx_recv.at[m], {"tensor": t_other}).wait_recv()

    own_c.wait()
    own_x.wait()
    load_f.wait()

    for h in range(heads):
        rows = pl.ds(h * HEAD_WIDTH, HEAD_WIDTH)
        which = layer_ref[t * heads + h]
        chosen = jnp.zeros((HEAD_WIDTH, half), F32)
        for layer in range(stored):
            chosen += fw[layer, rows, :].astype(F32) * (which == layer).astype(F32)
        fw[0, rows, :] = chosen.astype(BF16)

    shift = pl.multiple_of(t * width - start_of(t), 16)

    @pl.loop(0, tensor_n)
    def _(m):
        block[...] = lax.dot_general(qc[m], qx[m], TN, preferred_element_type=F32)
        weighted[m] = (fw[0].astype(F32) * block[pl.ds(shift, width), :]).astype(BF16)

    rows_n, rows_m = count * RB, tensor_n * RB
    row_id = lax.broadcasted_iota(jnp.int32, (rows_n, rows_m), 0)
    col_id = lax.broadcasted_iota(jnp.int32, (rows_n, rows_m), 1)
    same = (lax.rem(row_id, RB) == lax.rem(col_id, RB)).astype(F32)
    train_hot = (
        lax.broadcasted_iota(jnp.int32, (groups * ids_dev, count), 0) == tid_ref[...]
    ).astype(F32)
    query_hot = (
        lax.broadcasted_iota(jnp.int32, (rows_m, LANES), 1) == qid_ref[...]
    ).astype(F32)
    part[...] = jnp.zeros_like(part)
    for h in range(heads):
        acc[...] = jnp.zeros_like(acc)

        @pl.loop(0, HEAD_WIDTH // RB)
        def _(i):
            rows = pl.ds(pl.multiple_of(h * HEAD_WIDTH + i * RB, RB), RB)
            left = grad[:, rows, :].reshape(rows_n, half)
            right = weighted[:, rows, :].reshape(rows_m, half)
            acc[...] += lax.dot_general(left, right, NT, preferred_element_type=F32)

        kept = (acc[...] * same).reshape(count, RB, rows_m).sum(axis=1)
        by_query = jnp.dot(
            kept, query_hot, preferred_element_type=F32, precision=lax.Precision.HIGHEST
        )
        buckets = (
            jnp.dot(
                train_hot, by_query, preferred_element_type=F32, precision=lax.Precision.HIGHEST
            )
            * scale
        )
        for g in range(groups):
            part[g, h, 0:ids_dev, :] = buckets[g * ids_dev : (g + 1) * ids_dev, :]

    def exchange(d):
        g = lax.rem(me + d, groups)
        to = {"dp": g // fisher_n, "fisher": lax.rem(g, fisher_n)}
        return remote(part.at[g], got.at[d], part_send.at[d], part_recv.at[d], to)

    for d in range(1, groups):
        exchange(d).start()
    total = part[me]
    for d in range(1, groups):
        exchange(d).wait_recv()
        total += got[d]
    out_ref[...] = total

    for d in range(1, groups):
        exchange(d).wait_send()
    for k in c_order:

        @pl.when(on_line(k))
        def _(k=k):
            qc_first(k).wait_send()
            qc_to_dp(k).wait_send()
            qc_to_fisher(k).wait_send()

        @pl.when(jnp.logical_and(a != k % 2, f == (k // 2) % 2))
        def _(k=k):
            qc_to_fisher(k).wait_send()

    qx_partner().wait_send()
    for j in x_order:

        @pl.when(a == x_line(j, 0))
        def _(j=j):
            qx_first(j).wait_send()
            qx_to_dp(j).wait_send()
            qx_to_partner(j).wait_send()

        @pl.when(a != x_line(j, 0))
        def _(j=j):
            qx_to_partner(j).wait_send()


def local(axes, tx, tc, tids, qx, qc, qids, fw, layers):
    tensor_n, dp_n, fisher_n, ids_dev = axes
    count, seq, half = tx.shape
    width = tc.shape[2]
    heads = width // HEAD_WIDTH
    full = half * fisher_n
    scale = 1.0 / (seq * math.sqrt(HEAD_WIDTH * full))
    total_cols = qc.shape[2]
    win = 0
    for dest in range(tensor_n):
        lo = dest * width // LANES * LANES
        win = max(win, -(-(dest * width + width - lo) // LANES) * LANES)
    groups = dp_n * fisher_n
    sizes = (tensor_n, dp_n, fisher_n, win, ids_dev, scale)
    vmem = pl.BlockSpec(memory_space=pltpu.VMEM)
    hbm = pl.BlockSpec(memory_space=pl.ANY)
    dma = pltpu.SemaphoreType.DMA
    out = pl.pallas_call(
        functools.partial(kernel, sizes),
        out_shape=jax.ShapeDtypeStruct((heads, 8, LANES), F32),
        in_specs=[pl.BlockSpec(memory_space=pltpu.SMEM), hbm, hbm, hbm, hbm, hbm, vmem, vmem],
        out_specs=vmem,
        scratch_shapes=[
            pltpu.VMEM((count, seq, half), BF16),
            pltpu.VMEM((count, seq, width), BF16),
            pltpu.VMEM((count, width, half), BF16),
            pltpu.VMEM((tensor_n, seq, win), BF16),
            pltpu.VMEM((tensor_n, seq, half), BF16),
            pltpu.VMEM((tensor_n, width, half), BF16),
            pltpu.VMEM(fw.shape, BF16),
            pltpu.VMEM((win, half), F32),
            pltpu.VMEM((count * RB, tensor_n * RB), F32),
            pltpu.VMEM((groups, heads, 8, LANES), F32),
            pltpu.VMEM((groups, heads, 8, LANES), F32),
            dma((count,)),
            dma((count,)),
            dma,
            dma((2,)),
            dma((tensor_n,)),
            dma((3, tensor_n)),
            dma((tensor_n,)),
            dma((3, tensor_n // 2)),
            dma((groups,)),
            dma((groups,)),
        ],
        compiler_params=pltpu.CompilerParams(
            collective_id=0, has_side_effects=True, vmem_limit_bytes=60 * 1024 * 1024
        ),
    )(layers, tx, tc, qx, qc, fw, tids[None, :], jnp.repeat(qids, RB)[:, None])
    return jnp.transpose(out[:, :ids_dev, :QIDS], (1, 2, 0))


def solution(mesh):
    in_specs = (
        P("dp", None, "fisher"),
        P("dp", None, "tensor"),
        P("dp"),
        P("tensor", None, "fisher"),
        P("tensor", None, None),
        P(),
        P(None, "tensor", "fisher"),
        P(),
    )
    out_specs = P(("dp", "fisher"), None, "tensor")
    axes = (mesh.shape["tensor"], mesh.shape["dp"], mesh.shape["fisher"], 4)
    return jax.shard_map(
        functools.partial(local, axes),
        mesh=mesh,
        in_specs=in_specs,
        out_specs=out_specs,
        check_vma=False,
    )
```

time: 171 us -> 85.1 us (0.50)
  Pallas kernels: 0 us -> 82.2 us
  local copies, waits for them, and re-layouts: 60.8 us -> 2.72 us
  matrix products: 35.6 us -> 0 us
  other arithmetic: 27.4 us -> 0 us
  blocking collectives: 16 us -> 0 us
  between operations: 14.1 us -> 0.01 us
  waiting for transfers between devices: 9.24 us -> 0 us
  starting transfers between devices: 6.37 us -> 0 us
    pallas_call x0 -> x1, Pallas kernels: none -> 82.2 us  [local(): pl.pallas_call(functools.partial(kernel, sizes), out_shape=jax.ShapeDtype...]
    dot_general x4 -> x0, matrix products: 35.4 us -> none  [the longest x1 15.5 us: local(): jnp.einsum('nsr,nsd->nrd', train_cotangents, train_inputs, preferred_elem...]
    unnamed x14 -> x0, local copies, waits for them, and re-layouts: 31.9 us -> none
    reshape x2 -> x0, local copies, waits for them, and re-layouts: 25.5 us -> none  [the longest x1 18.1 us: local(): train_grad.reshape(count_train, local_heads, head_width * half_width)]
    unnamed x1 -> x0, other arithmetic: 24.6 us -> none
    unnamed x1 -> x0, blocking collectives: 16 us -> none
    all_to_all x1 -> x0, waiting for transfers between devices: 8.53 us -> none  [local(): lax.all_to_all(query_output_cotangents, 'tensor', split_axis=2, concat_ax...]
    all_to_all x1 -> x0, starting transfers between devices: 6.36 us -> none  [local(): lax.all_to_all(query_output_cotangents, 'tensor', split_axis=2, concat_ax...]
  transfers between devices with their start and end apart: 2 -> 0, of which waited for: 1 -> 0; matrix products, arithmetic and copies ran while one was open for 56% -> 0% of each run, Pallas kernels for 0% -> 0%
where the time goes in v1:
time: 85.1 us; the launch traced here: 84.9 us
  Pallas kernels  82.2 us (97%)
  local copies, waits for them, and re-layouts  2.72 us (3%)
    pallas_call x1, Pallas kernels, local(): pl.pallas_call(functools.partial(kernel, sizes), out_shape=jax.ShapeDtype...  82.2 us

profile of v1, /device:TPU:0, one launch (start us, length us, event | category | flops | bytes accessed | tf_op | source)
XLA Modules:
  0.0 84.9 jit_solution(13449382081595010284)
XLA Ops:
  0.0 0.7 broadcast_in_dim.7
  0.7 0.7 broadcast_in_dim_reshape.4.qid_ref
  1.4 82.2 %shard_map.82 = f32[2,8,128]{2,1,0:T(8,128)} custom-call(s32[16]{0:T(128)} %layer_ref.1, bf16[22,257,640]{2,1,0:T(8,128)(2,1)} %tx_hbm.1, bf16[22,257,480]{2,1,0:T(8,128)(2,1)} %tc_hbm.1, bf16[1,257,640]{2,1,0:T(8,128)(2,1)} %qx_hbm.1, bf16[1,257,3840]{2,1,0:T(8,128)(2,1)} %qc_hbm.1, bf16[2,480,640]{2,1,0:T(8,128)(2,1)} %fw_hbm.1, s32[1,22]{1,0:T(1,128)} %bitcast.3, ...), custom_call_target="tpu_custom_call" | custom-call | tf_op jit(solution)/shard_map/pallas_call | solution.py:351
  83.6 0.7 slice_bitcast_fusion
  84.3 0.6 copy.10

commit v2 on v1

--- a/solution.py
+++ b/solution.py
@@ -13,6 +13,7 @@
 QIDS = 16
 LANES = 128
 RB = 16
+CHUNKS = 4
 MESH = pl.DeviceIdType.MESH
 F32 = jnp.float32
 BF16 = jnp.bfloat16
@@ -46,6 +47,7 @@
     tc_sem,
     fw_sem,
     own_sem,
+    own_send,
     qc_recv,
     qc_send,
     qx_recv,
@@ -76,8 +78,14 @@
         first = lax.min((dest * width) // LANES * LANES, total_cols - win)
         return pl.multiple_of(first, LANES)
 
-    def window(dest):
-        return qc_hbm.at[0, :, pl.ds(start_of(dest), win)]
+    step = seq // (16 * CHUNKS) * 16
+
+    def rows_of(p):
+        return pl.ds(p * step, step if p + 1 < CHUNKS else seq - p * step)
+
+    def window(dest, p=None):
+        rows = slice(None) if p is None else rows_of(p)
+        return qc_hbm.at[0, rows, pl.ds(start_of(dest), win)]
 
     def remote(src, dst, send, recv, to):
         return pltpu.make_async_remote_copy(
@@ -108,75 +116,97 @@
     def load_c(n):
         return pltpu.make_async_copy(tc_hbm.at[n], tc.at[n], tc_sem.at[n])
 
+    pl.semaphore_wait(barrier, tensor_n - 1 + groups - 1)
+
+    def base_c(flip_a, flip_f):
+        return lax.rem(a + flip_a, 2) + 2 * lax.rem(f + flip_f, 2)
+
+    def slot(k):
+        return lax.rem(t + k, tensor_n)
+
+    def target(k):
+        return lax.rem(t + tensor_n - k, tensor_n)
+
+    def far(m):
+        return m // 2 != t // 2
+
+    def hop(buf, m, p, send, recv, to):
+        piece = buf.at[m, rows_of(p), :]
+        return remote(piece, piece, send, recv.at[m, p], to)
+
+    def qc_first(k, i, p):
+        return remote(
+            window(target(k), p),
+            qc.at[t, rows_of(p), :],
+            qc_send.at[0, i, p],
+            qc_recv.at[t, p],
+            {"tensor": target(k)},
+        )
+
+    def qc_partner():
+        return remote(
+            window(t_other), qc.at[t], own_send.at[0], qc_recv.at[t, 0], {"tensor": t_other}
+        )
+
+    def qc_to_dp(k, i, p):
+        return hop(qc, slot(k), p, qc_send.at[1, i, p], qc_recv, {"dp": dp_other})
+
+    def qc_to_fisher(k, i, p, via):
+        return hop(qc, slot(k), p, qc_send.at[via, i, p], qc_recv, {"fisher": f_other})
+
+    def base_x(flip):
+        return lax.rem(a + core + flip, 2)
+
+    def x_slot(j, side):
+        return 2 * lax.rem(t // 2 + j, chips) + lax.rem(core + side, 2)
+
+    def qx_first(j, i, p):
+        return remote(
+            qx_hbm.at[0, rows_of(p), :],
+            qx.at[t, rows_of(p), :],
+            qx_send.at[0, i, p],
+            qx_recv.at[t, p],
+            {"tensor": lax.rem(t + tensor_n - 2 * j, tensor_n)},
+        )
+
+    def qx_partner():
+        return remote(
+            qx_hbm.at[0], qx.at[t], own_send.at[1], qx_recv.at[t, 0], {"tensor": t_other}
+        )
+
+    def qx_to_partner(j, i, p, via):
+        return hop(qx, x_slot(j, 0), p, qx_send.at[via, i, p], qx_recv, {"tensor": t_other})
+
+    def qx_to_dp(j, i, p):
+        return hop(qx, x_slot(j, 0), p, qx_send.at[2, i, p], qx_recv, {"dp": dp_other})
+
+    c_steps, x_steps = tensor_n // 4, chips // 2
+    for p in range(CHUNKS):
+        for i in range(c_steps):
+            k = base_c(0, 0) + 4 * i
+
+            @pl.when(far(target(k)))
+            def _(k=k, i=i, p=p):
+                qc_first(k, i, p).start()
+
+    for i in range(x_steps):
+        j = base_x(0) + 2 * i
+
+        @pl.when(j > 0)
+        def _(j=j, i=i):
+            for p in range(CHUNKS):
+                qx_first(j, i, p).start()
+
+    qc_partner().start()
+    qx_partner().start()
     own_c.start()
     own_x.start()
+    load_f.start()
 
     @pl.loop(0, count)
     def _(n):
         load_x(n).start()
         load_c(n).start()
-
-    load_f.start()
-    pl.semaphore_wait(barrier, tensor_n - 1 + groups - 1)
-
-    def on_line(k):
-        return jnp.logical_and(a == k % 2, f == (k // 2) % 2)
-
-    def qc_first(k):
-        dest = lax.rem(t + tensor_n - k, tensor_n)
-        return remote(window(dest), qc.at[t], qc_send.at[0, k], qc_recv.at[t], {"tensor": dest})
-
-    def slot(k):
-        return lax.rem(t + k, tensor_n)
-
-    def qc_to_dp(k):
-        m = slot(k)
-        return remote(qc.at[m], qc.at[m], qc_send.at[1, k], qc_recv.at[m], {"dp": dp_other})
-
-    def qc_to_fisher(k):
-        m = slot(k)
-        return remote(qc.at[m], qc.at[m], qc_send.at[2, k], qc_recv.at[m], {"fisher": f_other})
-
-    def x_line(j, side):
-        source_core = lax.rem(core + side, 2)
-        return lax.rem(source_core + j, 2)
-
-    def x_slot(j, side):
-        return 2 * lax.rem(t // 2 + j, chips) + lax.rem(core + side, 2)
-
-    def qx_first(j):
-        dest = lax.rem(t + tensor_n - 2 * j, tensor_n)
-        return remote(qx_hbm.at[0], qx.at[t], qx_send.at[0, j], qx_recv.at[t], {"tensor": dest})
-
-    def qx_partner():
-        return remote(qx_hbm.at[0], qx.at[t], qx_send.at[0, 0], qx_recv.at[t], {"tensor": t_other})
-
-    def qx_to_partner(j):
-        m = x_slot(j, 0)
-        return remote(qx.at[m], qx.at[m], qx_send.at[1, j], qx_recv.at[m], {"tensor": t_other})
-
-    def qx_to_dp(j):
-        m = x_slot(j, 0)
-        return remote(qx.at[m], qx.at[m], qx_send.at[2, j], qx_recv.at[m], {"dp": dp_other})
-
-    x_order = list(range(1, chips))
-    c_order = list(range(1, tensor_n))
-    for i in range(max(len(x_order), len(c_order))):
-        if i < len(c_order):
-            k = c_order[i]
-
-            @pl.when(on_line(k))
-            def _(k=k):
-                qc_first(k).start()
-
-        if i < len(x_order):
-            j = x_order[i]
-
-            @pl.when(a == x_line(j, 0))
-            def _(j=j):
-                qx_first(j).start()
-
-    qx_partner().start()
 
     def train(lo, hi):
         @pl.loop(lo, hi)
@@ -185,76 +215,121 @@
             load_c(n).wait()
             grad[n] = lax.dot_general(tc[n], tx[n], TN, preferred_element_type=F32).astype(BF16)
 
-    def forward_c(k):
-        @pl.when(on_line(k))
+    def direct_c(i, p):
+        k = base_c(0, 0) + 4 * i
+
+        @pl.when(far(slot(k)))
         def _():
-            qc_to_dp(k).wait_recv()
-            qc_to_dp(k).start()
-            qc_to_fisher(k).start()
-
-    def forward_x(j):
-        @pl.when(a == x_line(j, 0))
+            qc_to_dp(k, i, p).wait_recv()
+            qc_to_dp(k, i, p).start()
+            qc_to_fisher(k, i, p, 2).start()
+
+    def direct_x(i, p):
+        j = base_x(0) + 2 * i
+
+        @pl.when(j > 0)
         def _():
-            qx_to_dp(j).wait_recv()
-            qx_to_dp(j).start()
-            qx_to_partner(j).start()
-
-    half_c = (len(c_order) + 1) // 2
-    cut = count // 3
-    train(0, cut)
-    for k in c_order[:half_c]:
-        forward_c(k)
-    for j in x_order[: (len(x_order) + 1) // 2]:
-        forward_x(j)
-    train(cut, 2 * cut)
-    for k in c_order[half_c:]:
-        forward_c(k)
-    for j in x_order[(len(x_order) + 1) // 2 :]:
-        forward_x(j)
-    train(2 * cut, count)
-
-    for k in c_order:
-
-        @pl.when(jnp.logical_and(a != k % 2, f == (k // 2) % 2))
-        def _(k=k):
-            qc_to_fisher(k).wait_recv()
-            qc_to_fisher(k).start()
-
-    for j in x_order:
-
-        @pl.when(a != x_line(j, 0))
-        def _(j=j):
-            qx_to_partner(j).wait_recv()
-            qx_to_partner(j).start()
-
-    for k in c_order:
-
-        @pl.when(f != (k // 2) % 2)
-        def _(k=k):
-            qc_to_fisher(k).wait_recv()
-
-    for j in range(chips):
+            qx_to_dp(j, i, p).wait_recv()
+            qx_to_dp(j, i, p).start()
+            qx_to_partner(j, i, p, 1).start()
+
+    def second_c(i, p):
+        k = base_c(1, 0) + 4 * i
+
+        @pl.when(far(slot(k)))
+        def _():
+            qc_to_fisher(k, i, p, 3).wait_recv()
+            qc_to_fisher(k, i, p, 3).start()
+
+    def second_x(i, p):
+        j = base_x(1) + 2 * i
+
+        @pl.when(j > 0)
+        def _():
+            qx_to_partner(j, i, p, 3).wait_recv()
+            qx_to_partner(j, i, p, 3).start()
+
+    def choose():
+        load_f.wait()
+        for h in range(heads):
+            rows = pl.ds(h * HEAD_WIDTH, HEAD_WIDTH)
+            which = layer_ref[t * heads + h]
+            chosen = jnp.zeros((HEAD_WIDTH, half), F32)
+            for layer in range(stored):
+                chosen += fw[layer, rows, :].astype(F32) * (which == layer).astype(F32)
+            fw[0, rows, :] = chosen.astype(BF16)
+
+    shift = pl.multiple_of(t * width - start_of(t), 16)
+
+    def weigh(m):
+        block[...] = lax.dot_general(qc[m], qx[m], TN, preferred_element_type=F32)
+        weighted[m] = (fw[0].astype(F32) * block[pl.ds(shift, width), :]).astype(BF16)
+
+    def last_c(flip, i):
+        k = base_c(flip, 1) + 4 * i
+
+        @pl.when(far(slot(k)))
+        def _():
+            for p in range(CHUNKS):
+                qc_to_fisher(k, i, p, 2).wait_recv()
+
+    def last_x(j):
         m = x_slot(j, 1)
-        remote(qx.at[m], qx.at[m], qx_send.at[1, j], qx_recv.at[m], {"tensor": t_other}).wait_recv()
-
+        for p in range(CHUNKS):
+            hop(qx, m, p, qx_send.at[0, 0, p], qx_recv, {"tensor": t_other}).wait_recv()
+
+    steps = CHUNKS * c_steps + 2
+    done = 0
+
+    def some_train():
+        nonlocal done
+        train(count * done // steps, count * (done + 1) // steps)
+        done += 1
+
+    some_train()
+    for p in range(CHUNKS):
+        for i in range(c_steps):
+            direct_c(i, p)
+        for i in range(c_steps):
+            if p > 0:
+                second_c(i, p - 1)
+            some_train()
+    choose()
+    for i in range(c_steps):
+        second_c(i, CHUNKS - 1)
     own_c.wait()
     own_x.wait()
-    load_f.wait()
-
-    for h in range(heads):
-        rows = pl.ds(h * HEAD_WIDTH, HEAD_WIDTH)
-        which = layer_ref[t * heads + h]
-        chosen = jnp.zeros((HEAD_WIDTH, half), F32)
-        for layer in range(stored):
-            chosen += fw[layer, rows, :].astype(F32) * (which == layer).astype(F32)
-        fw[0, rows, :] = chosen.astype(BF16)
-
-    shift = pl.multiple_of(t * width - start_of(t), 16)
-
-    @pl.loop(0, tensor_n)
-    def _(m):
-        block[...] = lax.dot_general(qc[m], qx[m], TN, preferred_element_type=F32)
-        weighted[m] = (fw[0].astype(F32) * block[pl.ds(shift, width), :]).astype(BF16)
+    for ref, sem in ((qc, qc_recv), (qx, qx_recv)):
+        remote(
+            ref.at[t_other],
+            ref.at[t_other],
+            own_send.at[0],
+            sem.at[t_other, 0],
+            {"tensor": t_other},
+        ).wait_recv()
+    some_train()
+    for p in range(CHUNKS):
+        direct_x(0, p)
+        if p > 0:
+            second_x(0, p - 1)
+    second_x(0, CHUNKS - 1)
+    weigh(t)
+    weigh(t_other)
+    for i in range(c_steps):
+        for flip in range(2):
+            last_c(flip, i)
+    for i in range(x_steps):
+        for p in range(CHUNKS if i + 1 < x_steps else 0):
+            direct_x(i + 1, p)
+            if p > 0:
+                second_x(i + 1, p - 1)
+        if i + 1 < x_steps:
+            second_x(i + 1, CHUNKS - 1)
+        for j in (2 * i, 2 * i + 1):
+            if j > 0:
+                last_x(j)
+                weigh(x_slot(j, 0))
+                weigh(x_slot(j, 1))
 
     rows_n, rows_m = count * RB, tensor_n * RB
     row_id = lax.broadcasted_iota(jnp.int32, (rows_n, rows_m), 0)
@@ -305,30 +380,41 @@
 
     for d in range(1, groups):
         exchange(d).wait_send()
-    for k in c_order:
-
-        @pl.when(on_line(k))
-        def _(k=k):
-            qc_first(k).wait_send()
-            qc_to_dp(k).wait_send()
-            qc_to_fisher(k).wait_send()
-
-        @pl.when(jnp.logical_and(a != k % 2, f == (k // 2) % 2))
-        def _(k=k):
-            qc_to_fisher(k).wait_send()
-
+    qc_partner().wait_send()
     qx_partner().wait_send()
-    for j in x_order:
-
-        @pl.when(a == x_line(j, 0))
-        def _(j=j):
-            qx_first(j).wait_send()
-            qx_to_dp(j).wait_send()
-            qx_to_partner(j).wait_send()
-
-        @pl.when(a != x_line(j, 0))
-        def _(j=j):
-            qx_to_partner(j).wait_send()
+    for p in range(CHUNKS):
+        for i in range(c_steps):
+            k = base_c(0, 0) + 4 * i
+
+            @pl.when(far(target(k)))
+            def _(k=k, i=i, p=p):
+                qc_first(k, i, p).wait_send()
+
+            @pl.when(far(slot(k)))
+            def _(k=k, i=i, p=p):
+                qc_to_dp(k, i, p).wait_send()
+                qc_to_fisher(k, i, p, 2).wait_send()
+
+            k = base_c(1, 0) + 4 * i
+
+            @pl.when(far(slot(k)))
+            def _(k=k, i=i, p=p):
+                qc_to_fisher(k, i, p, 3).wait_send()
+
+        for i in range(x_steps):
+            j = base_x(0) + 2 * i
+
+            @pl.when(j > 0)
+            def _(j=j, i=i, p=p):
+                qx_first(j, i, p).wait_send()
+                qx_to_dp(j, i, p).wait_send()
+                qx_to_partner(j, i, p, 1).wait_send()
+
+            j = base_x(1) + 2 * i
+
+            @pl.when(j > 0)
+            def _(j=j, i=i, p=p):
+                qx_to_partner(j, i, p, 3).wait_send()
 
 
 def local(axes, tx, tc, tids, qx, qc, qids, fw, layers):
@@ -369,10 +455,11 @@
             dma((count,)),
             dma,
             dma((2,)),
-            dma((tensor_n,)),
-            dma((3, tensor_n)),
-            dma((tensor_n,)),
-            dma((3, tensor_n // 2)),
+            dma((2,)),
+            dma((tensor_n, CHUNKS)),
+            dma((4, tensor_n // 4, CHUNKS)),
+            dma((tensor_n, CHUNKS)),
+            dma((4, tensor_n // 4, CHUNKS)),
             dma((groups,)),
             dma((groups,)),
         ],

time: 85.1 us -> 74.3 us (0.87)
  Pallas kernels: 82.2 us -> 71.3 us
    pallas_call x1, Pallas kernels: 82.2 us -> 71.3 us  [local(): pl.pallas_call(functools.partial(kernel, sizes), out_shape=jax.ShapeDtype...]
where the time goes in v2:
time: 74.3 us; the launch traced here: 74 us
  Pallas kernels  71.3 us (96%)
  local copies, waits for them, and re-layouts  2.72 us (4%)
    pallas_call x1, Pallas kernels, local(): pl.pallas_call(functools.partial(kernel, sizes), out_shape=jax.ShapeDtype...  71.3 us

profile of v2, /device:TPU:0, one launch (start us, length us, event | category | flops | bytes accessed | tf_op | source)
XLA Modules:
  0.0 74.0 jit_solution(15793959662838521642)
XLA Ops:
  0.0 0.7 broadcast_in_dim.7
  0.7 0.7 broadcast_in_dim_reshape.4.qid_ref
  1.4 71.3 %shard_map.82 = f32[2,8,128]{2,1,0:T(8,128)} custom-call(s32[16]{0:T(128)} %layer_ref.1, bf16[22,257,640]{2,1,0:T(8,128)(2,1)} %tx_hbm.1, bf16[22,257,480]{2,1,0:T(8,128)(2,1)} %tc_hbm.1, bf16[1,257,640]{2,1,0:T(8,128)(2,1)} %qx_hbm.1, bf16[1,257,3840]{2,1,0:T(8,128)(2,1)} %qc_hbm.1, bf16[2,480,640]{2,1,0:T(8,128)(2,1)} %fw_hbm.1, s32[1,22]{1,0:T(1,128)} %bitcast.3, ...), custom_call_target="tpu_custom_call" | custom-call | tf_op jit(solution)/shard_map/pallas_call | solution.py:437
  72.7 0.7 slice_bitcast_fusion
  73.4 0.6 copy.10
